TPU v7x, 512 devices: a whole 4x8x8 slice. The times are simulated.
512 devices in a mesh: row: 16 (over z, core), col: 32 (over y, x).
Axes of the slice: x: 4, y: 8, z: 8, core: 2. Of those that a mesh axis runs over, the one named last changes fastest.
Arguments:
- initial_voltage: float32 [16, 64, 128, 128], P('row', 'col'), may hold values from -6 to 6
- inject: float32 [16, 64, 128, 128], P('row', 'col'), may hold values from -6 to 6
- conduct: float32 [16, 64, 128, 128], P('row', 'col'), as said below
- capacitance: float32 [16, 64, 128], P('row', 'col'), may hold values from 1 to 4
- track_gain: float32 [16, 64, 2, 32], P('row', 'col'), may hold values from 0.3 to 3
- driver_tile: int32 [16, 32, 64], P('row', 'col'), may hold values from 0 to 1
- sink_net: int32 [16, 32, 32, 8], P('row', 'col'), may hold values from 0 to 63
- sink_count: int32 [16, 32, 32], P('row', 'col'), may hold values from 0 to 8, as said below
- sink_tile: int32 [16, 32, 32, 8], P('row', 'col'), may hold values from 0 to 1
- sink_node: int32 [16, 32, 32, 8], P('row', 'col'), may hold values from 0 to 127
- sink_gain: float32 [16, 32, 32, 8], P('row', 'col'), may hold values from 0.5 to 2
Outputs:
- voltage: float32 [16, 64, 128, 128], P('row', 'col')
Inputs may be any that keep to these rules, and one draw needn't show every extreme that they name: Slots k >= sink_count[d, s] are ignored; some receiving device takes all 8 slots from some source device in every draw. `conduct`: each tile's block is symmetric with non-positive entries off the diagonal and rows summing to zero.
All inputs are finite; a program needn't handle non-finite values.
Results may differ from a plain program's by a relative error of at most 0.0001.
Values sent between devices are 32-bit elements; how exact they have to be, the bound alone decides.
A program may use at most 64 MiB of HBM per device.

v0:
```python
import jax
import jax.numpy as jnp
from jax import lax
from jax.sharding import PartitionSpec as P

ITERS = 3
PRECISE = lax.Precision.HIGHEST


def padded_2(block, sides, width):
    for axis, dim in sides:
        count = lax.axis_size(axis)
        forward = [(i, i + 1) for i in range(count - 1)]
        backward = [(target, source) for source, target in forward]
        low = lax.ppermute(
            lax.slice_in_dim(block, block.shape[dim] - width, None, axis=dim), axis, forward
        )
        high = lax.ppermute(lax.slice_in_dim(block, 0, width, axis=dim), axis, backward)
        block = jnp.concatenate([low, block, high], axis=dim)
    return block


def shifted(block, axis, distance):
    devices = range(lax.axis_size(axis))
    route = [(i - distance, i) for i in devices if i - distance in devices]
    return lax.ppermute(block, axis, route)


def tile_inverse(conduct, capacitance):
    node_count = conduct.shape[-1]
    identity = jnp.eye(node_count, dtype=jnp.float32)
    whole_block = conduct + capacitance[..., None] * identity
    flat_blocks = whole_block.reshape((-1, node_count, node_count))
    factors = jnp.linalg.cholesky(flat_blocks)
    inverse = jax.vmap(lambda factor: jax.scipy.linalg.cho_solve((factor, True), identity))(factors)
    return inverse.reshape(whole_block.shape)


def apply_grid(voltage, conduct, capacitance, track_pad):
    edge_count = track_pad.shape[-1]
    inner_part = (
        jnp.einsum("rcij,rcjp->rcip", conduct, voltage, precision=PRECISE)
        + capacitance[..., None] * voltage
    )
    rim_cells = voltage[:, :, :edge_count, :]
    padded = padded_2(rim_cells, (("row", 0), ("col", 1)), 1)
    east_gain = track_pad[1:-1, 1:-1, 0][..., None]
    west_gain = track_pad[1:-1, :-2, 0][..., None]
    south_gain = track_pad[1:-1, 1:-1, 1][..., None]
    north_gain = track_pad[:-2, 1:-1, 1][..., None]
    track_flow = east_gain * (rim_cells - padded[1:-1, 2:]) + west_gain * (
        rim_cells - padded[1:-1, :-2]
    )
    track_flow = (
        track_flow
        + south_gain * (rim_cells - padded[2:, 1:-1])
        + north_gain * (rim_cells - padded[:-2, 1:-1])
    )
    return jnp.concatenate(
        [inner_part[:, :, :edge_count] + track_flow, inner_part[:, :, edge_count:]], axis=2
    )


def precondition(inverse, residual):
    return jnp.einsum("rcij,rcjp->rcip", inverse, residual, precision=PRECISE)


def inner_sum(left_vec, right_vec):
    return jnp.sum(left_vec * right_vec, axis=(0, 1, 2))


def residual_product(residual, precond):
    return lax.psum(inner_sum(residual, precond), ("row", "col"))


def solve_separate(right_side, initial, conduct, capacitance, track_pad, inverse):
    solution = initial
    residual = right_side - apply_grid(initial, conduct, capacitance, track_pad)
    precond = precondition(inverse, residual)
    direction = precond
    rz_now = residual_product(residual, precond)
    for sweep_idx in range(ITERS):
        applied = apply_grid(direction, conduct, capacitance, track_pad)
        curvature = lax.psum(inner_sum(direction, applied), ("row", "col"))
        step_size = rz_now / curvature
        solution = solution + step_size * direction
        residual = residual - step_size * applied
        precond = precondition(inverse, residual)
        rz_fresh = residual_product(residual, precond)
        direction = precond + rz_fresh / rz_now * direction
        rz_now = rz_fresh
    return solution


def driver_voltage(voltage, driver_tile):
    node_count = voltage.shape[2]
    flat_field = voltage.reshape((-1, voltage.shape[3]))
    net_count = driver_tile.shape[-1]
    row_index = (
        driver_tile.reshape(-1) * node_count + jnp.arange(net_count, dtype=jnp.int32) % node_count
    )
    return jnp.take(flat_field, row_index, axis=0)


def sink_current(values, sink_tile, sink_node, sink_gain, sink_count, node_count, tile_count):
    source_count, slot_count, pattern_count = values.shape
    live_slot = jnp.arange(slot_count, dtype=jnp.int32)[None, :] < sink_count.reshape(
        (source_count, 1)
    )
    weight = jnp.where(live_slot, sink_gain.reshape((source_count, slot_count)), jnp.float32(0.0))
    row_index = (sink_tile * node_count + sink_node).reshape(-1)
    scaled = (values * weight[..., None]).reshape((-1, pattern_count))
    injected = jnp.zeros((tile_count * node_count, pattern_count), jnp.float32)
    return injected.at[row_index].add(scaled)


def lower_rims(track_gain):
    west_piece = shifted(track_gain[:, -1:, 0, :], "col", 1)
    north_piece = shifted(track_gain[-1:, :, 1, :], "row", 1)
    track_pad = jnp.pad(track_gain, ((1, 1), (1, 1), (0, 0), (0, 0)))
    track_pad = track_pad.at[1:-1, 0, 0].set(west_piece[:, 0])
    return track_pad.at[0, 1:-1, 1].set(north_piece[0])


def local(
    initial_voltage,
    inject,
    conduct,
    capacitance,
    track_gain,
    driver_tile,
    sink_net,
    sink_count,
    sink_tile,
    sink_node,
    sink_gain,
):
    inverse = tile_inverse(conduct, capacitance)
    track_pad = lower_rims(track_gain)
    col_count = lax.axis_size("col")
    net_count = driver_tile.shape[-1]
    pattern_count = initial_voltage.shape[3]
    node_count = initial_voltage.shape[2]
    tile_count = initial_voltage.shape[0] * initial_voltage.shape[1]
    wanted = sink_net.reshape((sink_net.shape[2], sink_net.shape[3]))
    voltage = initial_voltage
    drivers = driver_voltage(voltage, driver_tile)
    gathered = lax.all_gather(drivers, "col", axis=0, tiled=True)
    offsets = jnp.arange(col_count, dtype=jnp.int32)[:, None] * net_count
    values = jnp.take(gathered, (wanted + offsets).reshape(-1), axis=0).reshape(
        wanted.shape + (pattern_count,)
    )
    injected = sink_current(
        values, sink_tile, sink_node, sink_gain, sink_count, node_count, tile_count
    )
    right_side = capacitance[..., None] * voltage + inject + injected.reshape(voltage.shape)
    voltage = solve_separate(right_side, voltage, conduct, capacitance, track_pad, inverse)
    return voltage


def solution(mesh):
    placed = (
        P("row", "col", None, None),
        P("row", "col", None, None),
        P("row", "col", None, None),
        P("row", "col", None),
        P("row", "col", None, None),
        P("row", "col", None),
        P("row", "col", None, None),
        P("row", "col", None),
        P("row", "col", None, None),
        P("row", "col", None, None),
        P("row", "col", None, None),
    )
    return jax.shard_map(
        local, mesh=mesh, in_specs=placed, out_specs=P("row", "col", None, None), check_vma=False
    )
```

profile of v0, /device:TPU:1, one launch (start us, length us, event | category | flops | bytes accessed | tf_op | source)
XLA Modules:
  0.0 707.5 jit_solution(17942465035946714458)
XLA Ops:
  6.5 1.1 copy.150
  7.6 8.8 %collective-permute-start.2 = (f32[1,2,32,128]{2,3,1,0:T(8,128)S(1)}, f32[1,2,32,128]{2,3,1,0:T(8,128)S(1)}, u32[]{:S(2)}, u32[]{:S(2)}) collective-permute-start(f32[1,2,32,128]{2,3,1,0:T(8,128)S(1)} %bitcast.150), channel_id=1, source_target_pairs={{32,0},{64,32},{96,64},{128,96},{160,128},{192,160},{224,192},{256... | collective-permute-start | bytes 98312 | tf_op jit(solution)/shard_map/ppermute | solution.py:18
  16.4 1.9 collective-permute-start.1
  18.4 1.3 collective-permute-start
  19.7 1.9 collective-permute-start.5
  29.1 1.3 collective-permute-start.3
  30.4 4.0 collective-permute-start.4
  34.5 1.1 collective-permute-done.4
  35.9 66.4 %all-gather.2.cloned.1.call-done = f32[2048,128]{1,0:T(8,128)} async-done(((f32[64,128]{1,0:T(8,128)}), f32[2048,128]{1,0:T(8,128)}) %all-gather.2.cloned.1.call-update) | async-done | bytes 1048592 | tf_op jit(solution)/shard_map/all_gather | solution.py:148
  102.3 3.4 scatter_custom_fusion
  106.0 23.5 %custom-call.11 = f32[2,128,128]{2,1,0:T(8,128)S(1)} custom-call(f32[2,128,128]{2,1,0:T(8,128)S(1)} %fusion.13), custom_call_target="Cholesky" | custom-call | tf_op jit(solution)/shard_map/jit(cholesky)/cholesky | solution.py:34
  129.8 19.7 %custom-call.12 = f32[2,1,128,128]{2,3,1,0:T(8,128)S(1)} custom-call(f32[2,1,128,128]{3,2,1,0:T(8,128)S(1)} %select_bitcast_fusion), custom_call_target="InvertDiagBlocksLowerTriangular" | custom-call | tf_op jit(solution)/shard_map/vmap(jit(_cho_solve))/triangular_solve | solution.py:35
  151.0 6.9 collective-permute-start.7
  157.9 3.2 collective-permute-start.6
  161.9 1.2 collective-permute-done.6
  163.1 1.3 collective-permute-start.8
  164.4 4.0 collective-permute-start.9
  170.1 103.8 %all-reduce.1 = (f32[128]{0:T(128)S(1)}, f32[128]{0:T(128)S(1)}) all-reduce(f32[128]{0:T(128)S(1)} %multiply_reduce_fusion, f32[128]{0:T(128)S(1)} %fusion.8), channel_id=1, replica_groups=mesh['row'=16,'col'=32] {'row','col'}, use_global_device_ids=true, to_apply=%region_4.5 | all-reduce | flops 256 | bytes 2048 | tf_op jit(solution)/shard_map/psum | solution.py:73
  274.5 95.4 %psum.44 = f32[128]{0:T(128)S(1)} all-reduce(f32[128]{0:T(128)S(1)} %get-tuple-element.56), channel_id=1, replica_groups=mesh['row'=16,'col'=32] {'row','col'}, use_global_device_ids=true, to_apply=%region_8.9 | all-reduce | flops 128 | bytes 1024 | tf_op jit(solution)/shard_map/psum | solution.py:73
  370.0 2.6 collective-permute-start.11
  372.6 3.3 collective-permute-start.10
  376.7 1.2 collective-permute-done.10
  377.9 1.3 collective-permute-start.12
  379.2 4.0 collective-permute-start.13
  384.8 102.0 %psum.45 = f32[128]{0:T(128)S(1)} all-reduce(f32[128]{0:T(128)S(1)} %fusion.10), channel_id=1, replica_groups=mesh['row'=16,'col'=32] {'row','col'}, use_global_device_ids=true, to_apply=%region_10.11 | all-reduce | flops 128 | bytes 1024 | tf_op jit(solution)/shard_map/psum | solution.py:84
  487.4 95.3 %psum.46 = f32[128]{0:T(128)S(1)} all-reduce(f32[128]{0:T(128)S(1)} %get-tuple-element.58), channel_id=1, replica_groups=mesh['row'=16,'col'=32] {'row','col'}, use_global_device_ids=true, to_apply=%region_12.13 | all-reduce | flops 128 | bytes 1024 | tf_op jit(solution)/shard_map/psum | solution.py:73
  582.7 2.6 collective-permute-start.15
  585.3 3.5 collective-permute-start.14
  589.6 1.2 collective-permute-done.14
  590.8 1.3 collective-permute-start.16
  592.1 4.0 collective-permute-start.17
  597.8 102.0 %psum.47 = f32[128]{0:T(128)S(1)} all-reduce(f32[128]{0:T(128)S(1)} %fusion.12), channel_id=1, replica_groups=mesh['row'=16,'col'=32] {'row','col'}, use_global_device_ids=true, to_apply=%region_14.15 | all-reduce | flops 128 | bytes 1024 | tf_op jit(solution)/shard_map/psum | solution.py:84
  (144 shorter events, 19.2 us)
Async XLA Ops:
  6.5 15.1 %copy-start.1 = (f32[1,2,128,128]{3,2,1,0:T(8,128)S(1)}, f32[1,2,128,128]{3,2,1,0:T(8,128)}, u32[]{:S(2)}) copy-start(f32[1,2,128,128]{3,2,1,0:T(8,128)} %param.15) | copy-start | bytes 393220
  6.5 11.8 %copy-start.4 = (f32[1,2,2,32]{3,2,1,0:T(2,128)S(1)}, f32[1,2,2,32]{3,2,1,0:T(2,128)}, u32[]{:S(2)}) copy-start(f32[1,2,2,32]{3,2,1,0:T(2,128)} %param.19) | copy-start | bytes 1540
  6.5 95.8 %all-gather.2.cloned.1.call-start = ((), (), s32[]{:S(2)}) async-start(), calls=%async_computation | async-start | bytes 1081344 | tf_op jit(solution)/shard_map/all_gather | solution.py:148
  7.6 21.3 %collective-permute-start.2 = (f32[1,2,32,128]{2,3,1,0:T(8,128)S(1)}, f32[1,2,32,128]{2,3,1,0:T(8,128)S(1)}, u32[]{:S(2)}, u32[]{:S(2)}) collective-permute-start(f32[1,2,32,128]{2,3,1,0:T(8,128)S(1)} %bitcast.150), channel_id=1, source_target_pairs={{32,0},{64,32},{96,64},{128,96},{160,128},{192,160},{224,192},{256... | collective-permute-start | bytes 98312 | tf_op jit(solution)/shard_map/ppermute | solution.py:18
  16.4 12.6 %collective-permute-start.1 = (f32[1,2,32,128]{2,3,1,0:T(8,128)S(1)}, f32[1,2,32,128]{2,3,1,0:T(8,128)S(1)}, u32[]{:S(2)}, u32[]{:S(2)}) collective-permute-start(f32[1,2,32,128]{2,3,1,0:T(8,128)S(1)} %bitcast.151), channel_id=1, source_target_pairs={{0,32},{32,64},{64,96},{96,128},{128,160},{160,192},{192,224},{224... | collective-permute-start | bytes 98312 | tf_op jit(solution)/shard_map/ppermute | solution.py:15
  18.4 10.5 %collective-permute-start = (f32[1,1,32]{2,1,0:T(1,128)S(1)}, f32[1,1,32]{2,1,0:T(1,128)S(1)}, u32[]{:S(2)}, u32[]{:S(2)}) collective-permute-start(f32[1,1,32]{2,1,0:T(1,128)S(1)} %slice_bitcast_fusion.1), channel_id=1, source_target_pairs={{0,1},{1,2},{2,3},{3,4},{4,5},{5,6},{6,7},{7,8},{8,9},{9,10},{10,1... | collective-permute-start | bytes 392 | tf_op jit(solution)/shard_map/ppermute | solution.py:26
  19.7 1.9 copy-start.10
  19.7 16.1 %collective-permute-start.5 = (f32[1,2,32]{2,1,0:T(2,128)S(1)}, f32[1,2,32]{2,1,0:T(2,128)S(1)}, u32[]{:S(2)}, u32[]{:S(2)}) collective-permute-start(f32[1,2,32]{2,1,0:T(2,128)S(1)} %bitcast.184), channel_id=1, source_target_pairs={{0,32},{32,64},{64,96},{96,128},{128,160},{160,192},{192,224},{224... | collective-permute-start | bytes 776 | tf_op jit(solution)/shard_map/ppermute | solution.py:26
  23.2 0.7 copy-start.5
  23.8 2.7 copy-start
  24.1 0.7 copy-start.9
  24.8 0.7 copy-start.6
  24.8 0.7 copy-start.7
  25.6 0.7 copy-start.8
  26.5 0.7 copy-start.3
  27.9 0.9 copy-start.2
  29.1 5.3 collective-permute-start.3
  30.4 5.2 collective-permute-start.4
  151.0 10.8 %collective-permute-start.7 = (f32[1,2,32,128]{2,3,1,0:T(8,128)S(1)}, f32[1,2,32,128]{2,3,1,0:T(8,128)S(1)}, u32[]{:S(2)}, u32[]{:S(2)}) collective-permute-start(f32[1,2,32,128]{2,3,1,0:T(8,128)S(1)} %bitcast.142), channel_id=1, source_target_pairs={{32,0},{64,32},{96,64},{128,96},{160,128},{192,160},{224,192},{256... | collective-permute-start | bytes 98312 | tf_op jit(solution)/shard_map/ppermute | solution.py:18
  157.9 5.1 collective-permute-start.6
  163.1 5.4 collective-permute-start.8
  164.4 5.2 collective-permute-start.9
  370.0 6.6 collective-permute-start.11
  372.6 5.2 collective-permute-start.10
  377.9 5.4 collective-permute-start.12
  379.2 5.2 collective-permute-start.13
  582.7 6.8 collective-permute-start.15
  585.3 5.4 collective-permute-start.14
  590.8 5.4 collective-permute-start.16
  592.1 5.2 collective-permute-start.17
Sparse Core Ops, SparseCore 0:
  23.1 79.1 all-gather.1
where the time goes:
time: 709 us; the launch traced here: 707 us
  blocking collectives  498 us (70%)
  waiting for transfers between devices  75.2 us (11%)
  starting transfers between devices  57 us (8%)
  other arithmetic  49.2 us (7%)
  between operations  14.1 us (2%)
  local copies, waits for them, and re-layouts  9.8 us (1%)
    psum x3, blocking collectives, residual_product(): return lax.psum(inner_sum(residual, precond), ('row', 'col'))  295 us
    psum x2, blocking collectives, solve_separate(): curvature = lax.psum(inner_sum(direction, applied), ('row', 'col'))  204 us
    all_gather x1, waiting for transfers between devices, local(): gathered = lax.all_gather(drivers, 'col', axis=0, tiled=True)  66.4 us
    ppermute x8, starting transfers between devices, padded_2(): lax.ppermute(lax.slice_in_dim(block, block.shape[dim] - width, None, axis...  27.8 us
    ppermute x8, starting transfers between devices, padded_2(): lax.ppermute(lax.slice_in_dim(block, 0, width, axis=dim), axis, backward)  26 us
    another operation x4, other arithmetic, tile_inverse(): factors = jnp.linalg.cholesky(flat_blocks)  23.6 us
    another operation x3, other arithmetic, tile_inverse(): jax.scipy.linalg.cho_solve((factor, True), identity)  19.8 us
  transfers between devices with their start and end apart: 19, of which 11 were waited for; matrix products, arithmetic and copies ran while one was open for 1% of the time, Pallas kernels for 0%

commit v1 on v0

--- a/solution.py
+++ b/solution.py
@@ -2,9 +2,16 @@
 import jax.numpy as jnp
 from jax import lax
 from jax.sharding import PartitionSpec as P
+from jax.lax import psum
 
 ITERS = 3
 PRECISE = lax.Precision.HIGHEST
+
+
+def _order_rounds(x_part):
+    for k in ("row", "col"):
+        x_part = psum(x_part, k)
+    return x_part
 
 
 def padded_2(block, sides, width):
@@ -70,7 +77,7 @@
 
 
 def residual_product(residual, precond):
-    return lax.psum(inner_sum(residual, precond), ("row", "col"))
+    return _order_rounds(inner_sum(residual, precond))
 
 
 def solve_separate(right_side, initial, conduct, capacitance, track_pad, inverse):

time: 709 us -> 797 us (1.12)
  blocking collectives: 498 us -> 562 us
  starting transfers between devices: 57 us -> 82.5 us
    psum x2 -> x3, blocking collectives: 204 us -> 312 us  [solve_separate(): curvature = lax.psum(inner_sum(direction, applied), ('row', 'col'))]
    psum x3 -> x6, blocking collectives: 295 us -> 249 us  [_order_rounds(): x_part = psum(x_part, k)]
    ppermute x8, starting transfers between devices: 26 us -> 54.4 us  [padded_2(): lax.ppermute(lax.slice_in_dim(block, 0, width, axis=dim), axis, backward)]
  transfers between devices with their start and end apart: 19 -> 19, of which waited for: 11 -> 10; matrix products, arithmetic and copies ran while one was open for 1% -> 1% of each run, Pallas kernels for 0% -> 0%
where the time goes in v1:
time: 797 us; the launch traced here: 795 us
  blocking collectives  562 us (71%)
  starting transfers between devices  82.5 us (10%)
  waiting for transfers between devices  74.4 us (9%)
  other arithmetic  49.2 us (6%)
  between operations  14.1 us (2%)
  local copies, waits for them, and re-layouts  9.81 us (1%)
    psum x3, blocking collectives, solve_separate(): curvature = lax.psum(inner_sum(direction, applied), ('row', 'col'))  312 us
    psum x6, blocking collectives, _order_rounds(): x_part = psum(x_part, k)  249 us
    all_gather x1, waiting for transfers between devices, local(): gathered = lax.all_gather(drivers, 'col', axis=0, tiled=True)  66.4 us
    ppermute x8, starting transfers between devices, padded_2(): lax.ppermute(lax.slice_in_dim(block, 0, width, axis=dim), axis, backward)  54.4 us
    ppermute x8, starting transfers between devices, padded_2(): lax.ppermute(lax.slice_in_dim(block, block.shape[dim] - width, None, axis...  24.9 us
    another operation x4, other arithmetic, tile_inverse(): factors = jnp.linalg.cholesky(flat_blocks)  23.6 us
    another operation x3, other arithmetic, tile_inverse(): jax.scipy.linalg.cho_solve((factor, True), identity)  19.8 us
  transfers between devices with their start and end apart: 19, of which 10 were waited for; matrix products, arithmetic and copies ran while one was open for 1% of the time, Pallas kernels for 0%

profile of v1, /device:TPU:1, one launch (start us, length us, event | category | flops | bytes accessed | tf_op | source)
XLA Modules:
  0.0 795.3 jit_solution(9317515298806243692)
XLA Ops:
  7.6 8.8 %collective-permute-start.2 = (f32[1,2,32,128]{2,3,1,0:T(8,128)S(1)}, f32[1,2,32,128]{2,3,1,0:T(8,128)S(1)}, u32[]{:S(2)}, u32[]{:S(2)}) collective-permute-start(f32[1,2,32,128]{2,3,1,0:T(8,128)S(1)} %bitcast.150), channel_id=1, source_target_pairs={{32,0},{64,32},{96,64},{128,96},{160,128},{192,160},{224,192},{256... | collective-permute-start | bytes 98312 | tf_op jit(solution)/shard_map/ppermute | solution.py:25
  16.4 1.9 collective-permute-start.1
  19.7 1.9 collective-permute-start.5
  29.1 1.3 collective-permute-start.3
  30.4 4.0 collective-permute-start.4
  35.9 66.4 %all-gather.2.cloned.1.call-done = f32[2048,128]{1,0:T(8,128)} async-done(((f32[64,128]{1,0:T(8,128)}), f32[2048,128]{1,0:T(8,128)}) %all-gather.2.cloned.1.call-update) | async-done | bytes 1048592 | tf_op jit(solution)/shard_map/all_gather | solution.py:155
  102.3 3.3 scatter_custom_fusion
  106.0 23.5 %custom-call.11 = f32[2,128,128]{2,1,0:T(8,128)S(1)} custom-call(f32[2,128,128]{2,1,0:T(8,128)S(1)} %fusion.13), custom_call_target="Cholesky" | custom-call | tf_op jit(solution)/shard_map/jit(cholesky)/cholesky | solution.py:41
  129.7 19.7 %custom-call.12 = f32[2,1,128,128]{2,3,1,0:T(8,128)S(1)} custom-call(f32[2,1,128,128]{3,2,1,0:T(8,128)S(1)} %select_bitcast_fusion), custom_call_target="InvertDiagBlocksLowerTriangular" | custom-call | tf_op jit(solution)/shard_map/vmap(jit(_cho_solve))/triangular_solve | solution.py:42
  151.0 7.0 collective-permute-start.7
  157.9 3.2 collective-permute-start.6
  163.1 1.3 collective-permute-start.8
  164.4 4.0 collective-permute-start.9
  168.5 25.7 %psum.63 = f32[128]{0:T(128)S(1)} all-reduce(f32[128]{0:T(128)S(1)} %multiply_reduce_fusion), channel_id=1, replica_groups=mesh['row'=16,'col'=32] {'row'}, use_global_device_ids=true, to_apply=%region_4.5 | all-reduce | flops 128 | bytes 1024 | tf_op jit(solution)/shard_map/psum | solution.py:13
  194.3 56.9 %psum.64 = f32[128]{0:T(128)S(1)} all-reduce(f32[128]{0:T(128)S(1)} %psum.63), channel_id=1, replica_groups=mesh['row'=16,'col'=32] {'col'}, use_global_device_ids=true, to_apply=%region_5.6 | all-reduce | flops 128 | bytes 1024 | tf_op jit(solution)/shard_map/psum | solution.py:13
  251.6 112.8 %psum.65 = f32[128]{0:T(128)S(1)} all-reduce(f32[128]{0:T(128)S(1)} %fusion.8), channel_id=1, replica_groups=mesh['row'=16,'col'=32] {'row','col'}, use_global_device_ids=true, to_apply=%region_7.8 | all-reduce | flops 128 | bytes 1024 | tf_op jit(solution)/shard_map/psum | solution.py:91
  365.0 23.6 %psum.66 = f32[128]{0:T(128)S(1)} all-reduce(f32[128]{0:T(128)S(1)} %get-tuple-element.54), channel_id=1, replica_groups=mesh['row'=16,'col'=32] {'row'}, use_global_device_ids=true, to_apply=%region_9.10 | all-reduce | flops 128 | bytes 1024 | tf_op jit(solution)/shard_map/psum | solution.py:13
  388.6 59.7 %psum.67 = f32[128]{0:T(128)S(1)} all-reduce(f32[128]{0:T(128)S(1)} %psum.66), channel_id=1, replica_groups=mesh['row'=16,'col'=32] {'col'}, use_global_device_ids=true, to_apply=%region_10.11 | all-reduce | flops 128 | bytes 1024 | tf_op jit(solution)/shard_map/psum | solution.py:13
  448.4 16.7 %collective-permute-start.11 = (f32[1,2,32,128]{2,3,1,0:T(8,128)S(1)}, f32[1,2,32,128]{2,3,1,0:T(8,128)S(1)}, u32[]{:S(2)}, u32[]{:S(2)}) collective-permute-start(f32[1,2,32,128]{2,3,1,0:T(8,128)S(1)} %bitcast.146), channel_id=1, source_target_pairs={{32,0},{64,32},{96,64},{128,96},{160,128},{192,160},{224,192},{256... | collective-permute-start | bytes 98312 | tf_op jit(solution)/shard_map/ppermute | solution.py:25
  465.2 1.9 collective-permute-start.10
  467.7 1.4 collective-permute-done.10
  469.2 1.3 collective-permute-start.12
  470.5 4.0 collective-permute-start.13
  476.2 99.8 %psum.68 = f32[128]{0:T(128)S(1)} all-reduce(f32[128]{0:T(128)S(1)} %fusion.10), channel_id=1, replica_groups=mesh['row'=16,'col'=32] {'row','col'}, use_global_device_ids=true, to_apply=%region_12.13 | all-reduce | flops 128 | bytes 1024 | tf_op jit(solution)/shard_map/psum | solution.py:91
  576.5 23.6 %psum.69 = f32[128]{0:T(128)S(1)} all-reduce(f32[128]{0:T(128)S(1)} %get-tuple-element.56), channel_id=1, replica_groups=mesh['row'=16,'col'=32] {'row'}, use_global_device_ids=true, to_apply=%region_14.15 | all-reduce | flops 128 | bytes 1024 | tf_op jit(solution)/shard_map/psum | solution.py:13
  600.1 59.7 %psum.70 = f32[128]{0:T(128)S(1)} all-reduce(f32[128]{0:T(128)S(1)} %psum.69), channel_id=1, replica_groups=mesh['row'=16,'col'=32] {'col'}, use_global_device_ids=true, to_apply=%region_15.16 | all-reduce | flops 128 | bytes 1024 | tf_op jit(solution)/shard_map/psum | solution.py:13
  659.9 16.7 %collective-permute-start.15 = (f32[1,2,32,128]{2,3,1,0:T(8,128)S(1)}, f32[1,2,32,128]{2,3,1,0:T(8,128)S(1)}, u32[]{:S(2)}, u32[]{:S(2)}) collective-permute-start(f32[1,2,32,128]{2,3,1,0:T(8,128)S(1)} %bitcast.153), channel_id=1, source_target_pairs={{32,0},{64,32},{96,64},{128,96},{160,128},{192,160},{224,192},{256... | collective-permute-start | bytes 98312 | tf_op jit(solution)/shard_map/ppermute | solution.py:25
  676.7 1.9 collective-permute-start.14
  679.2 1.4 collective-permute-done.14
  680.7 1.3 collective-permute-start.16
  682.0 4.0 collective-permute-start.17
  687.7 99.9 %psum.71 = f32[128]{0:T(128)S(1)} all-reduce(f32[128]{0:T(128)S(1)} %fusion.12), channel_id=1, replica_groups=mesh['row'=16,'col'=32] {'row','col'}, use_global_device_ids=true, to_apply=%region_17.18 | all-reduce | flops 128 | bytes 1024 | tf_op jit(solution)/shard_map/psum | solution.py:91
  (148 shorter events, 22.6 us)
Async XLA Ops:
  6.5 15.1 %copy-start.1 = (f32[1,2,128,128]{3,2,1,0:T(8,128)S(1)}, f32[1,2,128,128]{3,2,1,0:T(8,128)}, u32[]{:S(2)}) copy-start(f32[1,2,128,128]{3,2,1,0:T(8,128)} %param.15) | copy-start | bytes 393220
  6.5 11.8 %copy-start.4 = (f32[1,2,2,32]{3,2,1,0:T(2,128)S(1)}, f32[1,2,2,32]{3,2,1,0:T(2,128)}, u32[]{:S(2)}) copy-start(f32[1,2,2,32]{3,2,1,0:T(2,128)} %param.19) | copy-start | bytes 1540
  6.5 95.8 %all-gather.2.cloned.1.call-start = ((), (), s32[]{:S(2)}) async-start(), calls=%async_computation | async-start | bytes 1081344 | tf_op jit(solution)/shard_map/all_gather | solution.py:155
  7.6 21.3 %collective-permute-start.2 = (f32[1,2,32,128]{2,3,1,0:T(8,128)S(1)}, f32[1,2,32,128]{2,3,1,0:T(8,128)S(1)}, u32[]{:S(2)}, u32[]{:S(2)}) collective-permute-start(f32[1,2,32,128]{2,3,1,0:T(8,128)S(1)} %bitcast.150), channel_id=1, source_target_pairs={{32,0},{64,32},{96,64},{128,96},{160,128},{192,160},{224,192},{256... | collective-permute-start | bytes 98312 | tf_op jit(solution)/shard_map/ppermute | solution.py:25
  16.4 12.6 %collective-permute-start.1 = (f32[1,2,32,128]{2,3,1,0:T(8,128)S(1)}, f32[1,2,32,128]{2,3,1,0:T(8,128)S(1)}, u32[]{:S(2)}, u32[]{:S(2)}) collective-permute-start(f32[1,2,32,128]{2,3,1,0:T(8,128)S(1)} %bitcast.151), channel_id=1, source_target_pairs={{0,32},{32,64},{64,96},{96,128},{128,160},{160,192},{192,224},{224... | collective-permute-start | bytes 98312 | tf_op jit(solution)/shard_map/ppermute | solution.py:22
  18.4 10.5 %collective-permute-start = (f32[1,1,32]{2,1,0:T(1,128)S(1)}, f32[1,1,32]{2,1,0:T(1,128)S(1)}, u32[]{:S(2)}, u32[]{:S(2)}) collective-permute-start(f32[1,1,32]{2,1,0:T(1,128)S(1)} %slice_bitcast_fusion.1), channel_id=1, source_target_pairs={{0,1},{1,2},{2,3},{3,4},{4,5},{5,6},{6,7},{7,8},{8,9},{9,10},{10,1... | collective-permute-start | bytes 392 | tf_op jit(solution)/shard_map/ppermute | solution.py:33
  19.7 1.9 copy-start.10
  19.7 16.1 %collective-permute-start.5 = (f32[1,2,32]{2,1,0:T(2,128)S(1)}, f32[1,2,32]{2,1,0:T(2,128)S(1)}, u32[]{:S(2)}, u32[]{:S(2)}) collective-permute-start(f32[1,2,32]{2,1,0:T(2,128)S(1)} %bitcast.184), channel_id=1, source_target_pairs={{0,32},{32,64},{64,96},{96,128},{128,160},{160,192},{192,224},{224... | collective-permute-start | bytes 776 | tf_op jit(solution)/shard_map/ppermute | solution.py:33
  23.2 0.7 copy-start.5
  23.8 2.7 copy-start
  24.1 0.7 copy-start.9
  24.8 0.7 copy-start.6
  24.8 0.7 copy-start.7
  25.6 0.7 copy-start.8
  26.5 0.7 copy-start.3
  27.9 0.9 copy-start.2
  29.1 5.3 collective-permute-start.3
  30.4 5.2 collective-permute-start.4
  151.0 10.9 %collective-permute-start.7 = (f32[1,2,32,128]{2,3,1,0:T(8,128)S(1)}, f32[1,2,32,128]{2,3,1,0:T(8,128)S(1)}, u32[]{:S(2)}, u32[]{:S(2)}) collective-permute-start(f32[1,2,32,128]{2,3,1,0:T(8,128)S(1)} %bitcast.142), channel_id=1, source_target_pairs={{32,0},{64,32},{96,64},{128,96},{160,128},{192,160},{224,192},{256... | collective-permute-start | bytes 98312 | tf_op jit(solution)/shard_map/ppermute | solution.py:25
  157.9 5.1 collective-permute-start.6
  163.1 88.0 %collective-permute-start.8 = (f32[3,1,32,128]{3,2,1,0:T(8,128)S(1)}, f32[3,1,32,128]{3,2,1,0:T(8,128)S(1)}, u32[]{:S(2)}, u32[]{:S(2)}) collective-permute-start(f32[3,1,32,128]{3,2,1,0:T(8,128)S(1)} %get-tuple-element.43), channel_id=1, source_target_pairs={{1,0},{2,1},{3,2},{4,3},{5,4},{6,5},{7,6},{8,7},{9,8},{10,9},{11,1... | collective-permute-start | bytes 147464 | tf_op jit(solution)/shard_map/ppermute | solution.py:25
  164.4 86.7 %collective-permute-start.9 = (f32[3,1,32,128]{3,2,1,0:T(8,128)S(1)}, f32[3,1,32,128]{3,2,1,0:T(8,128)S(1)}, u32[]{:S(2)}, u32[]{:S(2)}) collective-permute-start(f32[3,1,32,128]{3,2,1,0:T(8,128)S(1)} %get-tuple-element.44), channel_id=1, source_target_pairs={{0,1},{1,2},{2,3},{3,4},{4,5},{5,6},{6,7},{7,8},{8,9},{9,10},{10,1... | collective-permute-start | bytes 147464 | tf_op jit(solution)/shard_map/ppermute | solution.py:22
  448.4 19.1 %collective-permute-start.11 = (f32[1,2,32,128]{2,3,1,0:T(8,128)S(1)}, f32[1,2,32,128]{2,3,1,0:T(8,128)S(1)}, u32[]{:S(2)}, u32[]{:S(2)}) collective-permute-start(f32[1,2,32,128]{2,3,1,0:T(8,128)S(1)} %bitcast.146), channel_id=1, source_target_pairs={{32,0},{64,32},{96,64},{128,96},{160,128},{192,160},{224,192},{256... | collective-permute-start | bytes 98312 | tf_op jit(solution)/shard_map/ppermute | solution.py:25
  465.2 3.9 collective-permute-start.10
  469.2 5.6 collective-permute-start.12
  470.5 5.3 collective-permute-start.13
  659.9 19.1 %collective-permute-start.15 = (f32[1,2,32,128]{2,3,1,0:T(8,128)S(1)}, f32[1,2,32,128]{2,3,1,0:T(8,128)S(1)}, u32[]{:S(2)}, u32[]{:S(2)}) collective-permute-start(f32[1,2,32,128]{2,3,1,0:T(8,128)S(1)} %bitcast.153), channel_id=1, source_target_pairs={{32,0},{64,32},{96,64},{128,96},{160,128},{192,160},{224,192},{256... | collective-permute-start | bytes 98312 | tf_op jit(solution)/shard_map/ppermute | solution.py:25
  676.7 3.9 collective-permute-start.14
  680.7 5.6 collective-permute-start.16
  682.0 5.3 collective-permute-start.17
Sparse Core Ops, SparseCore 0:
  23.1 79.1 all-gather.1
